TPU v7x, 32 devices: a whole 2x2x4 slice. The times are simulated.
32 devices in a mesh: leaf: 4 (over z), front: 8 (over y, x, core).
Axes of the slice: x: 2, y: 2, z: 4, core: 2. Of those that a mesh axis runs over, the one named last changes fastest.
Arguments:
- rhs_leaf: float32 [4, 2048, 64], P('leaf', 'front'), may hold values from -2.4 to 2.4
- diag_inv: bfloat16 [4, 8, 256, 256], P('leaf', 'front'), as said below
- sub_block: bfloat16 [4, 8, 256, 256], P('leaf', 'front'), as said below
- coupling: bfloat16 [4, 256, 2048], P('leaf', None, 'front'), may hold values from -0.25 to 0.25
- update_rows: int32 [4, 256], P('leaf'), may hold values from 0 to 1023, as said below
- rhs_sep: float32 [1024, 64], P('leaf'), may hold values from -6 to 6
- sep_inv: bfloat16 [1024, 1024], P('front', 'leaf'), as said below
Outputs:
- leaf_solution: float32 [4, 2048, 64], P('leaf', 'front')
- separator_solution: float32 [1024, 64], P('leaf')
Inputs may be any that keep to these rules, and one draw needn't show every extreme that they name: `update_rows`: within a group the 256 indices are distinct and increasing, and include the first and the last separator row. `diag_inv`: each 256 x 256 block is lower triangular. `sub_block`: each 256 x 256 block is lower triangular. `sep_inv`: lower triangular.
All inputs are finite; a program needn't handle non-finite values.
Results may differ from a plain program's by a relative error of at most 0.0003.
Values may be sent and summed in bfloat16 or wider, within the bound.
A program may use at most 64 MiB of HBM per device.

v0:
```python
import jax
import jax.numpy as jnp
from jax import lax
from jax.sharding import PartitionSpec as P

S = 1024
PRECISE = lax.Precision.HIGHEST


def carried_in(value, axis, join, neutral, backward):
    count, mine = (lax.axis_size(axis), lax.axis_index(axis))
    pieces = jax.tree.map(lambda part: lax.all_gather(part, axis), value)
    if backward:
        pieces = jax.tree.map(lambda part: part[::-1], pieces)
        mine = count - 1 - mine
    total = jax.tree.map(
        lambda part, zero: jnp.full_like(part, 0) + jnp.asarray(zero, part.dtype), value, neutral
    )

    def step(position, total):
        longer = join(total, jax.tree.map(lambda part: part[position], pieces))
        return jax.tree.map(lambda new, old: jnp.where(position < mine, new, old), longer, total)

    return lax.fori_loop(0, count - 1, step, total)


def shifted_2(value, axis, steps):
    count = lax.axis_size(axis)
    initial, last = (max(0, -steps), min(count, count - steps))
    return lax.ppermute(value, axis, [(source, source + steps) for source in range(initial, last)])


def product(left, right):
    return jnp.matmul(left, right, precision=PRECISE)


def narrow_product(left, right):
    return jnp.dot(left, right, preferred_element_type=jnp.float32)


def compose(earlier, later):
    return (product(later[0], earlier[0]), product(later[0], earlier[1]) + later[1])


def apply_maps(state, inputs):
    step_map, offset = inputs
    value = product(step_map, state) + offset
    return (value, value)


def forward_maps(carry, inputs):
    inverse, couple, right = inputs
    step_map = -narrow_product(inverse, couple)
    offset = product(inverse.astype(jnp.float32), right)
    mapped, shifted = carry
    return ((product(step_map, mapped), product(step_map, shifted) + offset), (step_map, offset))


def backward_maps(carry, inputs):
    inverse, couple, right = inputs
    step_map = -narrow_product(couple, inverse).T
    offset = product(inverse.astype(jnp.float32).T, right)
    mapped, shifted = carry
    return ((product(step_map, mapped), product(step_map, shifted) + offset), (step_map, offset))


def shards(rhs_leaf, diag_inv, sub_block, coupling, update_rows, rhs_sep, sep_inv):
    count = diag_inv.shape[1]
    width = diag_inv.shape[2]
    columns = rhs_leaf.shape[2]
    identity_w = jnp.eye(width, dtype=jnp.float32)
    zero_state = jnp.zeros((width, columns), jnp.float32)
    blocks = rhs_leaf[0].reshape(count, width, columns)
    (whole_map, whole_shift), (maps_fwd, offsets_fwd) = lax.scan(
        forward_maps, (identity_w, zero_state), (diag_inv[0], sub_block[0], blocks)
    )
    entering = carried_in(
        (whole_map, whole_shift), "front", compose, (identity_w, zero_state), False
    )
    _, solved_fwd = lax.scan(apply_maps, entering[1], (maps_fwd, offsets_fwd))
    forward_local = solved_fwd.reshape(count * width, columns)
    coupling_full = coupling[0].astype(jnp.float32)
    group_rows = product(coupling_full, forward_local)
    selector = (jnp.arange(S)[:, None] == update_rows[0][None, :]).astype(jnp.float32)
    update_term = product(selector, group_rows)
    gathered = lax.all_gather(sep_inv, "leaf", axis=1, tiled=True)
    whole_inv = lax.all_gather(gathered, "front", axis=0, tiled=True).astype(jnp.float32)
    rows_here = rhs_sep.shape[0]
    placed = lax.dynamic_update_slice_in_dim(
        jnp.zeros((S, columns), jnp.float32), rhs_sep, lax.axis_index("leaf") * rows_here, 0
    )
    leader = (lax.axis_index("front") == 0).astype(jnp.float32)
    reduced = lax.psum(leader * placed - update_term, ("leaf", "front"))
    sep_forward = product(whole_inv, reduced)
    solution_all = product(whole_inv.T, sep_forward)
    solution_sep = lax.dynamic_slice_in_dim(
        solution_all, lax.axis_index("leaf") * rows_here, rows_here, 0
    )
    selected_entries = product(selector.T, solution_all)
    adjusted = forward_local - product(coupling_full.T, selected_entries)
    next_first = shifted_2(sub_block[0, 0], "front", -1)
    following = jnp.concatenate([sub_block[0, 1:], next_first[None]], axis=0)
    adjusted_blocks = adjusted.reshape(count, width, columns)
    (back_map, back_shift), (maps_back, offsets_back) = lax.scan(
        backward_maps,
        (identity_w, zero_state),
        (diag_inv[0], following, adjusted_blocks),
        reverse=True,
    )
    arriving = carried_in((back_map, back_shift), "front", compose, (identity_w, zero_state), True)
    _, solved_back = lax.scan(apply_maps, arriving[1], (maps_back, offsets_back), reverse=True)
    return (solved_back, solution_sep)


def solution(mesh):
    return jax.shard_map(
        shards,
        mesh=mesh,
        in_specs=(
            P("leaf", "front", None),
            P("leaf", "front", None, None),
            P("leaf", "front", None, None),
            P("leaf", None, "front"),
            P("leaf", None),
            P("leaf", None),
            P("front", "leaf"),
        ),
        out_specs=(P("leaf", "front", None), P("leaf", None)),
        check_vma=False,
    )
```

profile of v0, /device:TPU:0, one launch (start us, length us, event | category | flops | bytes accessed | tf_op | source)
XLA Modules:
  0.0 245.7 jit_solution(13124845417316200062)
XLA Ops:
  8.1 1.1 convolution_negate_fusion
  10.2 1.3 collective-permute-start
  11.5 17.9 %all_gather.36 = bf16[128,1024]{1,0:T(8,128)(2,1)} all-gather(bf16[128,256]{1,0:T(8,128)(2,1)} %param.17), channel_id=1, replica_groups=mesh['leaf'=4,'front'=8] {'leaf'}, dimensions={1}, use_global_device_ids=true | all-gather | bytes 327680 | tf_op jit(solution)/shard_map/all_gather | solution.py:86
  29.5 1.1 fusion.29
  31.0 11.6 %all-gather.2 = f32[2048,64]{0,1:T(8,128)S(1)} all-gather(f32[256,64]{0,1:T(8,128)S(1)} %convolution_add_fusion.4), channel_id=4, replica_groups=mesh['leaf'=4,'front'=8] {'front'}, dimensions={0}, use_global_device_ids=true | all-gather | bytes 589824 | tf_op jit(solution)/shard_map/all_gather | solution.py:12
  43.2 10.0 %while.18 = (s32[]{:T(128)}, f32[256,64]{0,1:T(8,128)S(1)}, s32[]{:T(128)}, f32[8,256,256]{2,1,0:T(8,128)}, f32[8,256,64]{1,0,2:T(8,128)S(1)}, /*index=5*/s32[]{:T(128)}, s32[]{:T(128)}) while((s32[]{:T(128)}, f32[256,64]{0,1:T(8,128)S(1)}, s32[]{:T(128)}, f32[8,256,256]{2,1,0:T(8,128)}, f32[8,256,64]{1,0,2:T(8,128)S(1)}, ...), condition=%wide.region_1.2_spmd.clone, body=%wide.region_0.1_spmd.clone.sunk | while | flops 50397188 | bytes 788587 | solution.py:24
  43.3 1.3 fusion.67
  44.7 1.3 fusion.67
  46.1 1.3 fusion.67
  47.5 1.3 fusion.67
  48.9 1.3 fusion.67
  50.4 1.3 fusion.67
  51.8 1.3 fusion.67
  53.8 1.3 convolution_subtract_fusion
  55.2 1.0 fusion.24
  56.2 16.5 %all-gather.8.cloned.1.call-done = bf16[1024,1024]{1,0:T(8,128)(2,1)} async-done(((bf16[128,1024]{1,0:T(8,128)(2,1)}), bf16[1024,1024]{1,0:T(8,128)(2,1)}) %all-gather.8.cloned.1.call-update) | async-done | bytes 2097168 | tf_op jit(solution)/shard_map/all_gather | solution.py:87
  72.7 130.5 %all-reduce.2.cloned.1.call-done = f32[1024,64]{0,1:T(8,128)} async-done(((f32[1024,64]{0,1:T(8,128)}), f32[1024,64]{0,1:T(8,128)}) %all-reduce.2.cloned.1.call-update) | async-done | bytes 262160 | tf_op jit(solution)/shard_map/psum | solution.py:93
  203.3 3.7 %fusion.39 = f32[64,1024]{1,0:T(8,128)S(1)} fusion(f32[1024,64]{0,1:T(8,128)} %all-reduce.2.cloned.1.call-done, bf16[1024,1024]{1,0:T(8,128)(2,1)} %all-gather.8.cloned.1.call-done), kind=kOutput, calls=%fused_computation.56 | convolution fusion | flops 805306368 | bytes 2621440 | tf_op jit(solution)/shard_map/dot_general | solution.py:34
  207.0 1.2 fusion.40
  209.8 10.4 %all-gather.3 = f32[2048,64]{0,1:T(8,128)S(1)} all-gather(f32[256,64]{0,1:T(8,128)S(1)} %convolution_add_fusion.5), channel_id=5, replica_groups=mesh['leaf'=4,'front'=8] {'front'}, dimensions={0}, use_global_device_ids=true | all-gather | bytes 589824 | tf_op jit(solution)/shard_map/all_gather | solution.py:12
  221.0 12.4 %all-gather.10.cloned.1.call-done = f32[2048,256]{1,0:T(8,128)} async-done(((f32[256,256]{1,0:T(8,128)}), f32[2048,256]{1,0:T(8,128)}) %all-gather.10.cloned.1.call-update) | async-done | bytes 2097168 | tf_op jit(solution)/shard_map/all_gather | solution.py:12
  233.4 1.8 rev.6
  235.2 2.9 %while.19 = (s32[]{:T(128)}, f32[256,64]{0,1:T(8,128)S(1)}, s32[]{:T(128)}, f32[8,256,256]{2,1,0:T(8,128)S(1)}, f32[8,256,64]{1,2,0:T(8,128)S(1)}, /*index=5*/s32[]{:T(128)}, s32[]{:T(128)}) while((s32[]{:T(128)}, f32[256,64]{0,1:T(8,128)S(1)}, s32[]{:T(128)}, f32[8,256,256]{2,1,0:T(8,128)S(1)}, f32[8,256,64]{1,2,0:T(8,128)S(1)}, ...), condition=%wide.region_4.5_spmd.clone, body=%wide.region_3.4_spmd.clone.sunk | while | flops 50397188 | bytes 658023 | solution.py:24
  238.1 1.0 fusion.17
  (65 shorter events, 8.9 us)
Async XLA Ops:
  7.2 0.9 copy-start
  7.2 35.9 %all-gather.12.cloned.1.call-start = ((), (), s32[]{:S(2)}) async-start(), calls=%async_computation.3 | async-start | bytes 2359296 | tf_op jit(solution)/shard_map/all_gather | solution.py:12
  9.2 33.7 %copy-start.3 = (f32[256,64]{0,1:T(8,128)S(1)}, f32[256,64]{0,1:T(8,128)}, u32[]{:S(2)}) copy-start(f32[256,64]{0,1:T(8,128)} %param.16) | copy-start | bytes 196612
  10.2 62.6 %all-gather.8.cloned.1.call-start = ((), (), s32[]{:S(2)}) async-start(), calls=%async_computation.1 | async-start | bytes 2359296 | tf_op jit(solution)/shard_map/all_gather | solution.py:87
  10.2 32.6 %collective-permute-start = (bf16[256,256]{1,0:T(8,128)(2,1)}, bf16[256,256]{1,0:T(8,128)(2,1)S(1)}, u32[]{:S(2)}, u32[]{:S(2)}) collective-permute-start(bf16[256,256]{1,0:T(8,128)(2,1)} %bitcast.85), channel_id=1, source_target_pairs={{1,0},{2,1},{3,2},{4,3},{5,4},{6,5},{7,6},{9,8},{10,9},{11,10},{12... | collective-permute-start | bytes 393224 | tf_op jit(solution)/shard_map/ppermute | solution.py:30
  29.5 173.8 %all-reduce.2.cloned.1.call-start = ((), (), s32[]{:S(2)}) async-start(), calls=%async_computation | async-start | bytes 524288 | tf_op jit(solution)/shard_map/psum | solution.py:93
  43.1 10.4 %copy-start.2 = (bf16[1,256,256]{2,1,0:T(8,128)(2,1)S(1)}, bf16[1,256,256]{2,1,0:T(8,128)(2,1)}, u32[]{:S(2)}) copy-start(bf16[1,256,256]{2,1,0:T(8,128)(2,1)} %param.14) | copy-start | bytes 393220
  43.1 10.6 %copy-start.4 = (s32[1,256]{1,0:T(1,128)S(1)}, s32[1,256]{1,0:T(1,128)}, u32[]{:S(2)}) copy-start(s32[1,256]{1,0:T(1,128)} %param.15) | copy-start | bytes 3076
  55.2 178.2 %all-gather.10.cloned.1.call-start = ((), (), s32[]{:S(2)}) async-start(), calls=%async_computation.2 | async-start | bytes 2359296 | tf_op jit(solution)/shard_map/all_gather | solution.py:12
  72.7 134.2 %copy-start.1 = (bf16[1024,1024]{1,0:T(8,128)(2,1)S(1)}, bf16[1024,1024]{1,0:T(8,128)(2,1)}, u32[]{:S(2)}) copy-start(bf16[1024,1024]{1,0:T(8,128)(2,1)} %all-gather.8.cloned.1.call-done) | copy-start | bytes 6291460
Sparse Core Ops, SparseCore 0:
  10.3 31.7 all-gather.11
  44.0 28.7 all-gather.7
  78.2 124.9 all-reduce.1
  205.0 28.3 all-gather.9
where the time goes:
time: 246 us
  waiting for transfers between devices  160 us (65%)
  blocking collectives  40 us (16%)
  matrix products  26.2 us (11%)
  between operations  14 us (6%)
  local copies, waits for them, and re-layouts  4.04 us (2%)
    psum x1, waiting for transfers between devices, shards(): reduced = lax.psum(leader * placed - update_term, ('leaf', 'front'))  131 us
    dot_general x28, matrix products, product(): return jnp.matmul(left, right, precision=PRECISE)  24.9 us
    all_gather x2, blocking collectives, carried_in(): pieces = jax.tree.map(lambda part: lax.all_gather(part, axis), value)  22 us
    all_gather x1, blocking collectives, shards(): gathered = lax.all_gather(sep_inv, 'leaf', axis=1, tiled=True)  17.9 us
    all_gather x1, waiting for transfers between devices, shards(): lax.all_gather(gathered, 'front', axis=0, tiled=True).astype(jnp.float32)  16.5 us
    all_gather x2, waiting for transfers between devices, carried_in(): pieces = jax.tree.map(lambda part: lax.all_gather(part, axis), value)  12.5 us
  transfers between devices with their start and end apart: 5, of which 3 were waited for; matrix products, arithmetic and copies ran while one was open for 9% of the time, Pallas kernels for 0%

commit v1 on v0

--- a/solution.py
+++ b/solution.py
@@ -90,7 +90,7 @@
         jnp.zeros((S, columns), jnp.float32), rhs_sep, lax.axis_index("leaf") * rows_here, 0
     )
     leader = (lax.axis_index("front") == 0).astype(jnp.float32)
-    reduced = lax.psum(leader * placed - update_term, ("leaf", "front"))
+    reduced = jnp.sum(lax.all_gather(leader * placed - update_term, ("leaf", "front")), axis=0)
     sep_forward = product(whole_inv, reduced)
     solution_all = product(whole_inv.T, sep_forward)
     solution_sep = lax.dynamic_slice_in_dim(

time: 246 us -> 215 us (0.87)
  waiting for transfers between devices: 160 us -> 113 us
  local copies, waits for them, and re-layouts: 4.04 us -> 13 us
  matrix products: 26.2 us -> 31.4 us
    psum x1 -> x0, waiting for transfers between devices: 131 us -> none  [shards(): reduced = lax.psum(leader * placed - update_term, ('leaf', 'front'))]
    all_gather x0 -> x1, waiting for transfers between devices: none -> 79 us  [shards(): lax.all_gather(leader * placed - update_term, ('leaf', 'front'))]
    unnamed x11 -> x16, local copies, waits for them, and re-layouts: 1.04 us -> 9.14 us
    dot_general x28, matrix products: 24.9 us -> 30.1 us  [product(): return jnp.matmul(left, right, precision=PRECISE)]
    all_gather x1, blocking collectives: 17.9 us -> 14.8 us  [shards(): gathered = lax.all_gather(sep_inv, 'leaf', axis=1, tiled=True)]
    all_gather x2, blocking collectives: 22 us -> 24.8 us  [carried_in(): pieces = jax.tree.map(lambda part: lax.all_gather(part, axis), value)]
  transfers between devices with their start and end apart: 5 -> 5, of which waited for: 3 -> 5; matrix products, arithmetic and copies ran while one was open for 9% -> 12% of each run, Pallas kernels for 0% -> 0%
where the time goes in v1:
time: 215 us
  waiting for transfers between devices  113 us (53%)
  blocking collectives  39.5 us (18%)
  matrix products  31.4 us (15%)
  between operations  14 us (7%)
  local copies, waits for them, and re-layouts  13 us (6%)
    all_gather x1, waiting for transfers between devices, shards(): lax.all_gather(leader * placed - update_term, ('leaf', 'front'))  79 us
    dot_general x28, matrix products, product(): return jnp.matmul(left, right, precision=PRECISE)  30.1 us
    all_gather x2, blocking collectives, carried_in(): pieces = jax.tree.map(lambda part: lax.all_gather(part, axis), value)  24.8 us
    all_gather x1, waiting for transfers between devices, shards(): lax.all_gather(gathered, 'front', axis=0, tiled=True).astype(jnp.float32)  18.6 us
    all_gather x1, blocking collectives, shards(): gathered = lax.all_gather(sep_inv, 'leaf', axis=1, tiled=True)  14.8 us
    all_gather x2, waiting for transfers between devices, carried_in(): pieces = jax.tree.map(lambda part: lax.all_gather(part, axis), value)  13.7 us
    unnamed x16, local copies, waits for them, and re-layouts  9.14 us
  transfers between devices with their start and end apart: 5, of which 5 were waited for; matrix products, arithmetic and copies ran while one was open for 12% of the time, Pallas kernels for 0%

profile of v1, /device:TPU:0, one launch (start us, length us, event | category | flops | bytes accessed | tf_op | source)
XLA Modules:
  0.0 214.6 jit_solution(17451194447428540216)
XLA Ops:
  10.2 1.3 collective-permute-start
  11.5 2.2 %collective-permute-done = bf16[256,256]{1,0:T(8,128)(2,1)S(1)} collective-permute-done((bf16[256,256]{1,0:T(8,128)(2,1)}, bf16[256,256]{1,0:T(8,128)(2,1)S(1)}, u32[]{:S(2)}, u32[]{:S(2)}) %collective-permute-start) | collective-permute-done | bytes 131104 | tf_op jit(solution)/shard_map/ppermute | solution.py:30
  15.7 14.9 %all-gather.2 = f32[2048,64]{0,1:T(8,128)S(1)} all-gather(f32[256,64]{0,1:T(8,128)S(1)} %convolution_add_fusion.4), channel_id=4, replica_groups=mesh['leaf'=4,'front'=8] {'front'}, dimensions={0}, use_global_device_ids=true | all-gather | bytes 589824 | tf_op jit(solution)/shard_map/all_gather | solution.py:12
  30.9 10.8 %all-gather.14.cloned.1.call-done = f32[2048,256]{1,0:T(8,128)} async-done(((f32[256,256]{1,0:T(8,128)}), f32[2048,256]{1,0:T(8,128)}) %all-gather.14.cloned.1.call-update) | async-done | bytes 2097168 | tf_op jit(solution)/shard_map/all_gather | solution.py:12
  41.6 10.0 %while.18 = (s32[]{:T(128)}, f32[256,64]{0,1:T(8,128)S(1)}, s32[]{:T(128)}, f32[8,256,256]{2,1,0:T(8,128)}, f32[8,256,64]{1,0,2:T(8,128)S(1)}, /*index=5*/s32[]{:T(128)}, s32[]{:T(128)}) while((s32[]{:T(128)}, f32[256,64]{0,1:T(8,128)S(1)}, s32[]{:T(128)}, f32[8,256,256]{2,1,0:T(8,128)}, f32[8,256,64]{1,0,2:T(8,128)S(1)}, ...), condition=%wide.region_1.2_spmd.clone, body=%wide.region_0.1_spmd.clone.sunk | while | flops 50397188 | bytes 788579 | solution.py:24
  41.7 1.4 fusion.67
  43.2 1.3 fusion.67
  44.6 1.3 fusion.67
  46.0 1.3 fusion.67
  47.4 1.3 fusion.67
  48.9 1.3 fusion.67
  50.3 1.3 fusion.67
  52.3 1.4 convolution_subtract_fusion
  53.7 14.8 %all_gather.44 = bf16[128,1024]{1,0:T(8,128)(2,1)} all-gather(bf16[128,256]{1,0:T(8,128)(2,1)S(1)} %copy-done.3), channel_id=1, replica_groups=mesh['leaf'=4,'front'=8] {'leaf'}, dimensions={1}, use_global_device_ids=true | all-gather | bytes 327680 | tf_op jit(solution)/shard_map/all_gather | solution.py:86
  68.6 2.9 %all-gather.12.cloned.1.call-done = f32[2048,256]{1,0:T(8,128)} async-done(((f32[256,256]{1,0:T(8,128)}), f32[2048,256]{1,0:T(8,128)}) %all-gather.12.cloned.1.call-update) | async-done | bytes 2097168 | tf_op jit(solution)/shard_map/all_gather | solution.py:12
  71.4 1.8 rev.6
  73.3 79.0 %all-gather.16.cloned.1.call-done = f32[32768,64]{0,1:T(8,128)} async-done(((f32[1024,64]{0,1:T(8,128)}), f32[32768,64]{0,1:T(8,128)}) %all-gather.16.cloned.1.call-update) | async-done | bytes 8388624 | tf_op jit(solution)/shard_map/all_gather | solution.py:93
  152.2 8.1 %copy.16 = f32[8,8,32,1024]{3,2,1,0:T(8,128)S(1)} copy(f32[8,8,32,1024]{3,1,2,0:T(8,128)} %bitcast.84) | data formatting | bytes 16777216
  160.4 1.5 bitcast_reduce_fusion
  161.8 18.6 %all-gather.10.cloned.1.call-done = bf16[1024,1024]{1,0:T(8,128)(2,1)} async-done(((bf16[128,1024]{1,0:T(8,128)(2,1)}), bf16[1024,1024]{1,0:T(8,128)(2,1)}) %all-gather.10.cloned.1.call-update) | async-done | bytes 2097168 | tf_op jit(solution)/shard_map/all_gather | solution.py:87
  180.4 3.8 %fusion.39 = f32[64,1024]{1,0:T(8,128)S(1)} fusion(f32[1024,64]{0,1:T(8,128)S(1)} %bitcast_reduce_fusion, bf16[1024,1024]{1,0:T(8,128)(2,1)} %all-gather.10.cloned.1.call-done), kind=kOutput, calls=%fused_computation.57 | convolution fusion | flops 805306368 | bytes 2621440 | tf_op jit(solution)/shard_map/dot_general | solution.py:34
  187.6 9.8 %all-gather.4 = f32[2048,64]{0,1:T(8,128)S(1)} all-gather(f32[256,64]{0,1:T(8,128)S(1)} %convolution_add_fusion.5), channel_id=6, replica_groups=mesh['leaf'=4,'front'=8] {'front'}, dimensions={0}, use_global_device_ids=true | all-gather | bytes 589824 | tf_op jit(solution)/shard_map/all_gather | solution.py:12
  198.3 8.8 %while.19 = (s32[]{:T(128)}, f32[256,64]{0,1:T(8,128)S(1)}, s32[]{:T(128)}, f32[8,256,256]{2,1,0:T(8,128)S(1)}, f32[8,256,64]{1,2,0:T(8,128)}, /*index=5*/s32[]{:T(128)}, s32[]{:T(128)}) while((s32[]{:T(128)}, f32[256,64]{0,1:T(8,128)S(1)}, s32[]{:T(128)}, f32[8,256,256]{2,1,0:T(8,128)S(1)}, f32[8,256,64]{1,2,0:T(8,128)}, ...), condition=%wide.region_4.5_spmd.clone, body=%wide.region_3.4_spmd.clone.sunk | while | flops 50397188 | bytes 658015 | solution.py:24
  199.6 1.2 fusion.70
  (71 shorter events, 19.0 us)
Async XLA Ops:
  7.2 0.9 copy-start
  7.2 7.8 %copy-start.5 = (f32[1,256,64]{1,2,0:T(8,128)S(1)}, f32[1,256,64]{1,2,0:T(8,128)}, u32[]{:S(2)}) copy-start(f32[1,256,64]{1,2,0:T(8,128)} %param.11) | copy-start | bytes 196612
  7.2 34.4 %all-gather.14.cloned.1.call-start = ((), (), s32[]{:S(2)}) async-start(), calls=%async_computation.2 | async-start | bytes 2359296 | tf_op jit(solution)/shard_map/all_gather | solution.py:12
  10.2 20.7 %copy-start.4 = (f32[256,64]{0,1:T(8,128)S(1)}, f32[256,64]{0,1:T(8,128)}, u32[]{:S(2)}) copy-start(f32[256,64]{0,1:T(8,128)} %param.16) | copy-start | bytes 196612
  10.2 61.3 %all-gather.12.cloned.1.call-start = ((), (), s32[]{:S(2)}) async-start(), calls=%async_computation.1 | async-start | bytes 2359296 | tf_op jit(solution)/shard_map/all_gather | solution.py:12
  10.2 3.5 %collective-permute-start = (bf16[256,256]{1,0:T(8,128)(2,1)}, bf16[256,256]{1,0:T(8,128)(2,1)S(1)}, u32[]{:S(2)}, u32[]{:S(2)}) collective-permute-start(bf16[256,256]{1,0:T(8,128)(2,1)} %bitcast.91), channel_id=1, source_target_pairs={{1,0},{2,1},{3,2},{4,3},{5,4},{6,5},{7,6},{9,8},{10,9},{11,10},{12... | collective-permute-start | bytes 393224 | tf_op jit(solution)/shard_map/ppermute | solution.py:30
  15.0 137.3 %all-gather.16.cloned.1.call-start = ((), (), s32[]{:S(2)}) async-start(), calls=%async_computation.3 | async-start | bytes 8650752 | tf_op jit(solution)/shard_map/all_gather | solution.py:93
  41.6 10.4 %copy-start.2 = (bf16[1,256,256]{2,1,0:T(8,128)(2,1)S(1)}, bf16[1,256,256]{2,1,0:T(8,128)(2,1)}, u32[]{:S(2)}) copy-start(bf16[1,256,256]{2,1,0:T(8,128)(2,1)} %param.14) | copy-start | bytes 393220
  41.6 10.7 %copy-start.6 = (s32[1,256]{1,0:T(1,128)S(1)}, s32[1,256]{1,0:T(1,128)}, u32[]{:S(2)}) copy-start(s32[1,256]{1,0:T(1,128)} %param.15) | copy-start | bytes 3076
  41.6 12.1 %copy-start.3 = (bf16[128,256]{1,0:T(8,128)(2,1)S(1)}, bf16[128,256]{1,0:T(8,128)(2,1)}, u32[]{:S(2)}) copy-start(bf16[128,256]{1,0:T(8,128)(2,1)} %param.17) | copy-start | bytes 196612
  53.7 126.7 %all-gather.10.cloned.1.call-start = ((), (), s32[]{:S(2)}) async-start(), calls=%async_computation | async-start | bytes 2359296 | tf_op jit(solution)/shard_map/all_gather | solution.py:87
  180.4 3.8 %copy-start.1 = (bf16[1024,1024]{1,0:T(8,128)(2,1)S(1)}, bf16[1024,1024]{1,0:T(8,128)(2,1)}, u32[]{:S(2)}) copy-start(bf16[1024,1024]{1,0:T(8,128)(2,1)} %all-gather.10.cloned.1.call-done) | copy-start | bytes 6291460
Sparse Core Ops, SparseCore 0:
  10.3 31.2 all-gather.13
  43.5 27.8 all-gather.11
  74.4 77.8 all-gather.15
  154.0 26.3 all-gather.9
